TPU v7x, 256 devices: a whole 4x4x8 slice. The times are simulated.
256 devices in a mesh: group: 8 (over y, core), tile: 32 (over z, x).
Axes of the slice: x: 4, y: 4, z: 8, core: 2. Of those that a mesh axis runs over, the one named last changes fastest.
Arguments:
- radiance: bfloat16 [224, 3072, 1024], P(None, 'tile', 'group'), may hold values from -200 to 200
- valid_mask: int32 [3072, 1024], P('tile', 'group'), may hold values 0 or 1
Outputs:
- whitened: bfloat16 [224, 3072, 1024], P(None, 'tile', 'group')
- whitened_cov: float32 [224, 224], replicated
All inputs are finite; a program needn't handle non-finite values. No bound on the sum of `valid_mask` on one device may be relied on, other than what follows from the above.
Results may differ from a plain program's by a relative error of at most 0.0058.
Values may be sent and summed in bfloat16 or wider, within the bound.
No kernel may reach another device: no remote copies, remote signals or barrier semaphores. Data moves between devices by JAX's collectives and lax.ppermute only.
A program may use at most 128 MiB of HBM per device.

v0:
```python
import jax
import jax.numpy as jnp
from jax import lax
from jax.sharding import PartitionSpec as P


def padded_2(block, sides, width):
    for axis, dim in sides:
        count = lax.axis_size(axis)
        forward = [(i, i + 1) for i in range(count - 1)]
        backward = [(target, source) for source, target in forward]
        low = lax.ppermute(
            lax.slice_in_dim(block, block.shape[dim] - width, None, axis=dim), axis, forward
        )
        high = lax.ppermute(lax.slice_in_dim(block, 0, width, axis=dim), axis, backward)
        block = jnp.concatenate([low, block, high], axis=dim)
    return block


def smooth_noise(padded, rows, cols):
    field = padded.astype(jnp.float32)
    row_smooth = (
        field[:, 0:rows]
        + 4.0 * field[:, 1 : rows + 1]
        + 6.0 * field[:, 2 : rows + 2]
        + 4.0 * field[:, 3 : rows + 3]
        + field[:, 4 : rows + 4]
    ) / 16.0
    smooth = (
        row_smooth[:, :, 0:cols]
        + 4.0 * row_smooth[:, :, 1 : cols + 1]
        + 6.0 * row_smooth[:, :, 2 : cols + 2]
        + 4.0 * row_smooth[:, :, 3 : cols + 3]
        + row_smooth[:, :, 4 : cols + 4]
    ) / 16.0
    centre = field[:, 2 : rows + 2, 2 : cols + 2]
    noise = centre - 0.5 * (
        field[:, 1 : rows + 1, 2 : cols + 2] + field[:, 3 : rows + 3, 2 : cols + 2]
    )
    return (smooth, noise)


def finish(signal_moment, noise_moment, signal_first, noise_first, count):
    signal_cov = (signal_moment - jnp.outer(signal_first, signal_first) / count) / (count - 1.0)
    noise_cov = (noise_moment - jnp.outer(noise_first, noise_first) / count) / (count - 1.0)
    lower = jnp.linalg.cholesky(noise_cov)
    identity = jnp.eye(signal_first.shape[0], dtype=jnp.float32)
    inverse_lower = jax.scipy.linalg.solve_triangular(lower, identity, lower=True)
    left = jnp.dot(inverse_lower, signal_cov, precision=lax.Precision.HIGHEST)
    whitened_cov = jnp.dot(left, inverse_lower.T, precision=lax.Precision.HIGHEST)
    return (inverse_lower, whitened_cov)


def body(radiance, valid_mask):
    bands, rows, cols = radiance.shape
    padded = padded_2(radiance, (("group", 2), ("tile", 1)), 2)
    smooth, noise = smooth_noise(padded, rows, cols)
    weight = valid_mask.astype(jnp.float32)[None]
    signal_masked = smooth * weight
    noise_masked = noise * weight
    signal_first = jnp.sum(signal_masked, axis=(1, 2))
    noise_first = jnp.sum(noise_masked, axis=(1, 2))
    count = jnp.sum(weight)
    signal_flat = signal_masked.astype(jnp.bfloat16).reshape(bands, rows * cols)
    noise_flat = noise_masked.astype(jnp.bfloat16).reshape(bands, rows * cols)
    dims = (((1,), (1,)), ((), ()))
    signal_moment = lax.dot_general(
        signal_flat, signal_flat, dims, preferred_element_type=jnp.float32
    )
    noise_moment = lax.dot_general(noise_flat, noise_flat, dims, preferred_element_type=jnp.float32)
    count_column = jnp.full((bands,), count, jnp.float32)
    block = jnp.concatenate([signal_moment, noise_moment], axis=1)
    side = jnp.stack([signal_first, noise_first, count_column], axis=1)
    total_block, total_side = lax.psum((block, side), ("group", "tile"))
    signal_total = total_block[:, :bands]
    noise_total = total_block[:, bands:]
    count_total = total_side[0, 2]
    signal_sum = total_side[:, 0]
    inverse_lower, whitened_cov = finish(
        signal_total, noise_total, signal_sum, total_side[:, 1], count_total
    )
    inverse_cast = inverse_lower.astype(jnp.bfloat16)
    mean_signal = signal_sum / count_total
    centered = (
        (weight * (smooth - mean_signal[:, None, None]))
        .astype(jnp.bfloat16)
        .reshape(bands, rows * cols)
    )
    product = jnp.dot(inverse_cast, centered, preferred_element_type=jnp.float32)
    whitened = product.astype(jnp.bfloat16).reshape(bands, rows, cols)
    return (whitened, whitened_cov)


def solution(mesh):
    return jax.shard_map(
        body,
        mesh=mesh,
        in_specs=(P(None, "tile", "group"), P("tile", "group")),
        out_specs=(P(None, "tile", "group"), P()),
        check_vma=False,
    )
```

profile of v0, /device:TPU:6, one launch (start us, length us, event | category | flops | bytes accessed | tf_op | source)
XLA Modules:
  0.0 533.3 jit_solution(12199069908704797337)
XLA Ops:
  7.2 10.8 %fusion.46 = (bf16[224,96,2]{2,1,0:T(8,128)(2,1)}, bf16[224,96,2]{2,1,0:T(8,128)(2,1)}) fusion(bf16[224,96,128]{2,1,0:T(8,128)(2,1)} %param.2), kind=kLoop, calls=%fused_computation.90 | loop fusion | bytes 344064 | tf_op jit(solution)/shard_map/slice | solution.py:13
  18.0 5.8 %copy.33 = bf16[224,96,2]{0,1,2:T(8,128)(2,1)S(1)} copy(bf16[224,96,2]{2,1,0:T(8,128)(2,1)} %get-tuple-element.29) | data formatting | bytes 172032
  23.9 1.3 collective-permute-start.1
  25.2 5.8 %copy.32 = bf16[224,96,2]{0,1,2:T(8,128)(2,1)S(1)} copy(bf16[224,96,2]{2,1,0:T(8,128)(2,1)} %get-tuple-element.28) | data formatting | bytes 172032
  31.0 3.0 collective-permute-start
  34.0 9.3 %copy.19 = bf16[224,96,128]{0,2,1:T(8,128)(2,1)} copy(bf16[224,96,128]{2,1,0:T(8,128)(2,1)} %param.2) | data formatting | bytes 11010048 | tf_op args[0]
  44.2 1.1 pad_maximum_fusion.6
  45.3 3.7 collective-permute-start.2
  49.0 2.3 collective-permute-start.3
  51.3 0.7 pad.18.clone
  52.0 1.4 collective-permute-done.2
  53.5 6.0 %collective-permute-done.3 = bf16[224,2,132]{0,2,1:T(8,128)(2,1)S(1)} collective-permute-done((bf16[224,2,132]{0,2,1:T(8,128)(2,1)S(1)}, bf16[224,2,132]{0,2,1:T(8,128)(2,1)S(1)}, u32[]{:S(2)}, u32[]{:S(2)}) %collective-permute-start.3) | collective-permute-done | bytes 118304 | tf_op jit(solution)/shard_map/ppermute | solution.py:15
  59.5 8.8 %maximum_convert_fusion = f32[224,100,132]{0,2,1:T(8,128)S(1)} fusion(bf16[224,2,132]{0,2,1:T(8,128)(2,1)S(1)} %collective-permute-done.3, bf16[224,96,2]{0,2,1:T(2,128)(2,1)S(1)} %copy.20, bf16[224,96,128]{0,2,1:T(8,128)(2,1)} %copy.19, bf16[224,96,2]{0,2,1:T(2,128)(2,1)S(1)} %copy.18, bf16[224,2,132]{0,2,1:T(8,128)(2,1)S(1)} %collective-permute-done.2), kind=kLoop, calls=%fused_computation.23 | loop fusion | flops 29568000 | bytes 17740800 | tf_op jit(solution)/shard_map/convert_element_type | solution.py:21
  68.3 8.0 %fusion = f32[224,96,132]{0,2,1:T(8,128)} fusion(f32[224,100,132]{0,2,1:T(8,128)S(1)} %maximum_convert_fusion), kind=kLoop, calls=%fused_computation.2 | loop fusion | flops 22708224 | bytes 68124672 | tf_op jit(solution)/shard_map/div | solution.py:22
  76.3 7.3 %fusion.44 = (f32[224]{0:T(256)S(1)}, bf16[224,96,128]{0,2,1:T(8,128)(2,1)}) fusion(f32[96,128]{1,0:T(8,128)S(1)} %convert_element_type.23, f32[224,100,132]{0,2,1:T(8,128)S(1)} %maximum_convert_fusion), kind=kLoop, calls=%fused_computation.89 | loop fusion | flops 16514848 | bytes 38585216 | tf_op jit(solution)/shard_map/reduce_sum | solution.py:62
  83.6 29.3 %multiply_reduce_fusion = (f32[224]{0:T(256)S(1)}, f32[224,96,128]{0,2,1:T(8,128)}) fusion(f32[96,128]{1,0:T(8,128)S(1)} %get-tuple-element.35, f32[224,96,132]{0,2,1:T(8,128)} %fusion), kind=kLoop, calls=%fused_computation.21 | loop fusion | flops 24772384 | bytes 66110336 | tf_op jit(solution)/shard_map/reduce_sum | solution.py:61
  113.0 79.0 %psum.15 = f32[224,3]{0,1:T(4,128)S(1)} all-reduce(f32[224,3]{0,1:T(4,128)S(1)} %maximum_maximum_fusion), channel_id=1, replica_groups=mesh['group'=8,'tile'=32] {'group','tile'}, use_global_device_ids=true, to_apply=%region_4.0 | all-reduce | flops 672 | bytes 5376 | tf_op jit(solution)/shard_map/psum | solution.py:74
  192.5 13.9 %fusion.18 = f32[224,224]{0,1:T(8,128)S(1)} fusion(f32[224,96,128]{0,2,1:T(8,128)} %get-tuple-element.23, f32[96,128]{1,0:T(8,128)S(1)} %get-tuple-element.35), kind=kOutput, calls=%fused_computation.30 | convolution fusion | flops 1238630400 | bytes 11259904 | tf_op jit(solution)/shard_map/dot_general | solution.py:67
  206.4 2.4 fusion.15
  208.9 0.8 pad_maximum_fusion
  210.3 8.6 %multiply_convert_fusion = bf16[224,96,128]{0,2,1:T(8,128)(2,1)} fusion(f32[224,96,128]{0,2,1:T(8,128)} %get-tuple-element.23, f32[224]{0:T(256)S(1)} %broadcast_divide_fusion, f32[96,128]{1,0:T(8,128)S(1)} %convert_element_type.23), kind=kLoop, calls=%fused_computation.20 | loop fusion | flops 11010048 | bytes 16565120 | tf_op jit(solution)/shard_map/convert_element_type | solution.py:86
  219.6 237.9 %all-reduce.5.cloned.1.call-done = f32[224,448]{0,1:T(8,128)} async-done(((f32[224,448]{0,1:T(8,128)}), f32[224,448]{0,1:T(8,128)}) %all-reduce.5.cloned.1.call-update) | async-done | bytes 401424 | tf_op jit(solution)/shard_map/psum | solution.py:74
  457.5 1.7 fusion.22
  459.4 1.7 fusion.23
  461.1 11.7 %cholesky.51 = f32[128,128]{1,0:T(8,128)S(1)} custom-call(f32[128,128]{1,0:T(8,128)S(1)} %cholesky.124), custom_call_target="Cholesky" | custom-call | tf_op jit(solution)/shard_map/jit(cholesky)/cholesky | solution.py:46
  473.5 9.8 %custom-call.15 = f32[1,128,128]{1,2,0:T(8,128)S(1)} custom-call(f32[1,128,128]{2,1,0:T(8,128)S(1)} %get-tuple-element.31), custom_call_target="InvertDiagBlocksLowerTriangular" | custom-call | tf_op jit(solution)/shard_map/jit(cholesky)/cholesky | solution.py:46
  483.8 8.8 %cholesky.110 = f32[96,96]{1,0:T(8,128)S(1)} custom-call(f32[96,96]{1,0:T(8,128)S(1)} %convolution_subtract_fusion.1), custom_call_target="Cholesky" | custom-call | tf_op jit(solution)/shard_map/jit(cholesky)/cholesky | solution.py:46
  494.6 20.0 %custom-call.16 = f32[2,128,128]{1,2,0:T(8,128)S(1)} custom-call(f32[2,128,128]{2,1,0:T(8,128)S(1)} %pad_maximum_fusion.7), custom_call_target="InvertDiagBlocksLowerTriangular" | custom-call | tf_op jit(solution)/shard_map/jit(_solve_triangular)/triangular_solve | solution.py:48
  515.7 4.8 fusion.14
  520.5 1.3 fusion.20
  521.8 1.0 fusion.26
  522.8 3.6 copy.34
  (40 shorter events, 5.2 us)
Async XLA Ops:
  7.2 450.4 %all-reduce.5.cloned.1.call-start = ((), (), s32[]{:S(2)}) async-start(), calls=%async_computation | async-start | bytes 917504 | tf_op jit(solution)/shard_map/psum | solution.py:74
  18.0 25.3 %copy-start.1 = (s32[96,128]{1,0:T(8,128)S(1)}, s32[96,128]{1,0:T(8,128)}, u32[]{:S(2)}) copy-start(s32[96,128]{1,0:T(8,128)} %param.3) | copy-start | bytes 147460
  23.9 20.1 %collective-permute-start.1 = (bf16[224,96,2]{0,1,2:T(8,128)(2,1)S(1)}, bf16[224,96,2]{0,1,2:T(8,128)(2,1)S(1)}, u32[]{:S(2)}, u32[]{:S(2)}) collective-permute-start(bf16[224,96,2]{0,1,2:T(8,128)(2,1)S(1)} %copy.33), channel_id=1, source_target_pairs={{32,0},{64,32},{96,64},{128,96},{160,128},{192,160},{224,192},{33,... | collective-permute-start | bytes 258056 | tf_op jit(solution)/shard_map/ppermute | solution.py:15
  31.0 13.1 %collective-permute-start = (bf16[224,96,2]{0,1,2:T(8,128)(2,1)S(1)}, bf16[224,96,2]{0,1,2:T(8,128)(2,1)S(1)}, u32[]{:S(2)}, u32[]{:S(2)}) collective-permute-start(bf16[224,96,2]{0,1,2:T(8,128)(2,1)S(1)} %copy.32), channel_id=1, source_target_pairs={{0,32},{32,64},{64,96},{96,128},{128,160},{160,192},{192,224},{1,3... | collective-permute-start | bytes 258056 | tf_op jit(solution)/shard_map/ppermute | solution.py:12
  45.3 8.2 %collective-permute-start.2 = (bf16[224,2,132]{0,2,1:T(8,128)(2,1)S(1)}, bf16[224,2,132]{0,2,1:T(8,128)(2,1)S(1)}, u32[]{:S(2)}, u32[]{:S(2)}) collective-permute-start(bf16[224,2,132]{0,2,1:T(8,128)(2,1)S(1)} %get-tuple-element.26), channel_id=1, source_target_pairs={{0,1},{1,2},{2,3},{3,4},{4,5},{5,6},{6,7},{7,8},{8,9},{9,10},{10,1... | collective-permute-start | bytes 354824 | tf_op jit(solution)/shard_map/ppermute | solution.py:12
  49.0 10.5 %collective-permute-start.3 = (bf16[224,2,132]{0,2,1:T(8,128)(2,1)S(1)}, bf16[224,2,132]{0,2,1:T(8,128)(2,1)S(1)}, u32[]{:S(2)}, u32[]{:S(2)}) collective-permute-start(bf16[224,2,132]{0,2,1:T(8,128)(2,1)S(1)} %get-tuple-element.27), channel_id=1, source_target_pairs={{1,0},{2,1},{3,2},{4,3},{5,4},{6,5},{7,6},{8,7},{9,8},{10,9},{11,1... | collective-permute-start | bytes 354824 | tf_op jit(solution)/shard_map/ppermute | solution.py:15
  112.9 93.5 %slice-start = ((s8[6291456]{0:T(1024)(128)(4,1)}), s8[2097152]{0:T(1024)(128)(4,1)S(1)}, s32[]{:S(2)}) async-start(s8[6291456]{0:T(1024)(128)(4,1)} %bitcast.44), calls=%async_computation.1 | async-start | bytes 4194304
  192.5 13.9 %slice-start.1 = ((s8[6291456]{0:T(1024)(128)(4,1)}), s8[4194304]{0:T(1024)(128)(4,1)S(1)}, s32[]{:S(2)}) async-start(s8[6291456]{0:T(1024)(128)(4,1)} %bitcast.44), calls=%async_computation.2 | async-start | bytes 8388608
  457.5 63.0 %copy-start = (f32[224,448]{0,1:T(8,128)S(1)}, f32[224,448]{0,1:T(8,128)}, u32[]{:S(2)}) copy-start(f32[224,448]{0,1:T(8,128)} %all-reduce.5.cloned.1.call-done) | copy-start | bytes 1204228
Sparse Core Ops, SparseCore 0:
  209.8 247.6 all-reduce.4
where the time goes:
time: 534 us; the launch traced here: 533 us
  waiting for transfers between devices  245 us (46%)
  other arithmetic  120 us (22%)
  blocking collectives  79 us (15%)
  local copies, waits for them, and re-layouts  37 us (7%)
  matrix products  24.9 us (5%)
  between operations  16.2 us (3%)
  starting transfers between devices  10.4 us (2%)
    psum x1, waiting for transfers between devices, body(): total_block, total_side = lax.psum((block, side), ('group', 'tile'))  238 us
    psum x1, blocking collectives, body(): total_block, total_side = lax.psum((block, side), ('group', 'tile'))  79 us
    another operation x7, other arithmetic, finish(): lower = jnp.linalg.cholesky(noise_cov)  31.7 us
    reduce_sum x1, other arithmetic, body(): signal_first = jnp.sum(signal_masked, axis=(1, 2))  29.3 us
    unnamed x12, local copies, waits for them, and re-layouts  24.5 us
    another operation x6, other arithmetic, finish(): jax.scipy.linalg.solve_triangular(lower, identity, lower=True)  20.1 us
    dot_general x1, matrix products, body(): lax.dot_general(signal_flat, signal_flat, dims, preferred_element_type=jn...  13.9 us
    slice x1, local copies, waits for them, and re-layouts, padded_2(): lax.slice_in_dim(block, block.shape[dim] - width, None, axis=dim)  10.8 us
  transfers between devices with their start and end apart: 5, of which 3 were waited for; matrix products, arithmetic and copies ran while one was open for 5% of the time, Pallas kernels for 0%

commit v1 on v0

--- a/solution.py
+++ b/solution.py
@@ -71,7 +71,7 @@
     count_column = jnp.full((bands,), count, jnp.float32)
     block = jnp.concatenate([signal_moment, noise_moment], axis=1)
     side = jnp.stack([signal_first, noise_first, count_column], axis=1)
-    total_block, total_side = lax.psum((block, side), ("group", "tile"))
+    total_block, total_side = lax.psum(lax.psum((block, side), "group"), "tile")
     signal_total = total_block[:, :bands]
     noise_total = total_block[:, bands:]
     count_total = total_side[0, 2]

time: 534 us -> 508 us (0.951)
  waiting for transfers between devices: 245 us -> 217 us
    psum x1 -> x2, waiting for transfers between devices: 238 us -> 210 us  [body(): total_block, total_side = lax.psum(lax.psum((block, side), 'group'), 'tile')]
    psum x1 -> x2, blocking collectives: 79 us -> 79.5 us  [body(): total_block, total_side = lax.psum(lax.psum((block, side), 'group'), 'tile')]
  transfers between devices with their start and end apart: 5 -> 6, of which waited for: 3 -> 4; matrix products, arithmetic and copies ran while one was open for 5% -> 5% of each run, Pallas kernels for 0% -> 0%
where the time goes in v1:
time: 508 us; the launch traced here: 506 us
  waiting for transfers between devices  217 us (43%)
  other arithmetic  120 us (24%)
  blocking collectives  79.5 us (16%)
  local copies, waits for them, and re-layouts  36.9 us (7%)
  matrix products  24.9 us (5%)
  between operations  16.2 us (3%)
  starting transfers between devices  10.7 us (2%)
    psum x2, waiting for transfers between devices, body(): total_block, total_side = lax.psum(lax.psum((block, side), 'group'), 'tile')  210 us
    psum x2, blocking collectives, body(): total_block, total_side = lax.psum(lax.psum((block, side), 'group'), 'tile')  79.5 us
    another operation x7, other arithmetic, finish(): lower = jnp.linalg.cholesky(noise_cov)  31.7 us
    reduce_sum x1, other arithmetic, body(): signal_first = jnp.sum(signal_masked, axis=(1, 2))  29.3 us
    unnamed x12, local copies, waits for them, and re-layouts  24.5 us
    another operation x6, other arithmetic, finish(): jax.scipy.linalg.solve_triangular(lower, identity, lower=True)  20.1 us
    dot_general x1, matrix products, body(): lax.dot_general(signal_flat, signal_flat, dims, preferred_element_type=jn...  13.9 us
    slice x1, local copies, waits for them, and re-layouts, padded_2(): lax.slice_in_dim(block, block.shape[dim] - width, None, axis=dim)  10.8 us
  transfers between devices with their start and end apart: 6, of which 4 were waited for; matrix products, arithmetic and copies ran while one was open for 5% of the time, Pallas kernels for 0%

profile of v1, /device:TPU:6, one launch (start us, length us, event | category | flops | bytes accessed | tf_op | source)
XLA Modules:
  0.0 505.9 jit_solution(13301875045395722235)
XLA Ops:
  7.2 10.8 %fusion.46 = (bf16[224,96,2]{2,1,0:T(8,128)(2,1)}, bf16[224,96,2]{2,1,0:T(8,128)(2,1)}) fusion(bf16[224,96,128]{2,1,0:T(8,128)(2,1)} %param.2), kind=kLoop, calls=%fused_computation.90 | loop fusion | bytes 344064 | tf_op jit(solution)/shard_map/slice | solution.py:13
  18.0 5.8 %copy.33 = bf16[224,96,2]{0,1,2:T(8,128)(2,1)S(1)} copy(bf16[224,96,2]{2,1,0:T(8,128)(2,1)} %get-tuple-element.29) | data formatting | bytes 172032
  23.8 1.3 collective-permute-start.1
  25.1 5.8 %copy.32 = bf16[224,96,2]{0,1,2:T(8,128)(2,1)S(1)} copy(bf16[224,96,2]{2,1,0:T(8,128)(2,1)} %get-tuple-element.28) | data formatting | bytes 172032
  31.0 3.0 collective-permute-start
  34.0 9.3 %copy.19 = bf16[224,96,128]{0,2,1:T(8,128)(2,1)} copy(bf16[224,96,128]{2,1,0:T(8,128)(2,1)} %param.2) | data formatting | bytes 11010048 | tf_op args[0]
  44.2 1.1 pad_maximum_fusion.6
  45.2 3.7 collective-permute-start.2
  49.0 2.3 collective-permute-start.3
  52.0 1.4 collective-permute-done.2
  53.4 6.0 %collective-permute-done.3 = bf16[224,2,132]{0,2,1:T(8,128)(2,1)S(1)} collective-permute-done((bf16[224,2,132]{0,2,1:T(8,128)(2,1)S(1)}, bf16[224,2,132]{0,2,1:T(8,128)(2,1)S(1)}, u32[]{:S(2)}, u32[]{:S(2)}) %collective-permute-start.3) | collective-permute-done | bytes 118304 | tf_op jit(solution)/shard_map/ppermute | solution.py:15
  59.5 8.8 %maximum_convert_fusion = f32[224,100,132]{0,2,1:T(8,128)S(1)} fusion(bf16[224,2,132]{0,2,1:T(8,128)(2,1)S(1)} %collective-permute-done.3, bf16[224,96,2]{0,2,1:T(2,128)(2,1)S(1)} %copy.20, bf16[224,96,128]{0,2,1:T(8,128)(2,1)} %copy.19, bf16[224,96,2]{0,2,1:T(2,128)(2,1)S(1)} %copy.18, bf16[224,2,132]{0,2,1:T(8,128)(2,1)S(1)} %collective-permute-done.2), kind=kLoop, calls=%fused_computation.23 | loop fusion | flops 29568000 | bytes 17740800 | tf_op jit(solution)/shard_map/convert_element_type | solution.py:21
  68.2 8.0 %fusion = f32[224,96,132]{0,2,1:T(8,128)} fusion(f32[224,100,132]{0,2,1:T(8,128)S(1)} %maximum_convert_fusion), kind=kLoop, calls=%fused_computation.2 | loop fusion | flops 22708224 | bytes 68124672 | tf_op jit(solution)/shard_map/div | solution.py:22
  76.3 7.3 %fusion.44 = (f32[224]{0:T(256)S(1)}, bf16[224,96,128]{0,2,1:T(8,128)(2,1)}) fusion(f32[96,128]{1,0:T(8,128)S(1)} %convert_element_type.23, f32[224,100,132]{0,2,1:T(8,128)S(1)} %maximum_convert_fusion), kind=kLoop, calls=%fused_computation.89 | loop fusion | flops 16514848 | bytes 38585216 | tf_op jit(solution)/shard_map/reduce_sum | solution.py:62
  83.6 29.3 %multiply_reduce_fusion = (f32[224]{0:T(256)S(1)}, f32[224,96,128]{0,2,1:T(8,128)}) fusion(f32[96,128]{1,0:T(8,128)S(1)} %get-tuple-element.35, f32[224,96,132]{0,2,1:T(8,128)} %fusion), kind=kLoop, calls=%fused_computation.21 | loop fusion | flops 24772384 | bytes 66110336 | tf_op jit(solution)/shard_map/reduce_sum | solution.py:61
  113.0 12.6 %psum.30 = f32[224,3]{0,1:T(4,128)S(1)} all-reduce(f32[224,3]{0,1:T(4,128)S(1)} %maximum_maximum_fusion), channel_id=1, replica_groups=mesh['group'=8,'tile'=32] {'group'}, use_global_device_ids=true, to_apply=%region_5.0 | all-reduce | flops 672 | bytes 5376 | tf_op jit(solution)/shard_map/psum | solution.py:74
  125.5 67.0 %psum.31 = f32[224,3]{0,1:T(4,128)S(1)} all-reduce(f32[224,3]{0,1:T(4,128)S(1)} %psum.30), channel_id=1, replica_groups=mesh['group'=8,'tile'=32] {'tile'}, use_global_device_ids=true, to_apply=%region_6.0 | all-reduce | flops 672 | bytes 5376 | tf_op jit(solution)/shard_map/psum | solution.py:74
  193.0 13.9 %fusion.18 = f32[224,224]{0,1:T(8,128)S(1)} fusion(f32[224,96,128]{0,2,1:T(8,128)} %get-tuple-element.23, f32[96,128]{1,0:T(8,128)S(1)} %get-tuple-element.35), kind=kOutput, calls=%fused_computation.30 | convolution fusion | flops 1238630400 | bytes 11259904 | tf_op jit(solution)/shard_map/dot_general | solution.py:67
  206.9 2.4 fusion.15
  211.7 69.8 %all-reduce.6.cloned.1.call-done = f32[224,448]{0,1:T(8,128)} async-done(((f32[224,448]{0,1:T(8,128)}), f32[224,448]{0,1:T(8,128)}) %all-reduce.6.cloned.1.call-update) | async-done | bytes 401424 | tf_op jit(solution)/shard_map/psum | solution.py:74
  281.6 8.6 %multiply_convert_fusion = bf16[224,96,128]{0,2,1:T(8,128)(2,1)} fusion(f32[224,96,128]{0,2,1:T(8,128)} %get-tuple-element.23, f32[224]{0:T(256)S(1)} %broadcast_divide_fusion, f32[96,128]{1,0:T(8,128)S(1)} %convert_element_type.23), kind=kLoop, calls=%fused_computation.20 | loop fusion | flops 11010048 | bytes 16565120 | tf_op jit(solution)/shard_map/convert_element_type | solution.py:86
  290.2 140.0 %all-reduce.8.cloned.1.call-done = f32[224,448]{0,1:T(8,128)} async-done(((f32[224,448]{0,1:T(8,128)}), f32[224,448]{0,1:T(8,128)}) %all-reduce.8.cloned.1.call-update) | async-done | bytes 401424 | tf_op jit(solution)/shard_map/psum | solution.py:74
  430.2 1.7 fusion.22
  432.1 1.7 fusion.23
  433.8 11.7 %cholesky.51 = f32[128,128]{1,0:T(8,128)S(1)} custom-call(f32[128,128]{1,0:T(8,128)S(1)} %cholesky.124), custom_call_target="Cholesky" | custom-call | tf_op jit(solution)/shard_map/jit(cholesky)/cholesky | solution.py:46
  446.2 9.8 %custom-call.15 = f32[1,128,128]{1,2,0:T(8,128)S(1)} custom-call(f32[1,128,128]{2,1,0:T(8,128)S(1)} %get-tuple-element.31), custom_call_target="InvertDiagBlocksLowerTriangular" | custom-call | tf_op jit(solution)/shard_map/jit(cholesky)/cholesky | solution.py:46
  456.5 8.8 %cholesky.110 = f32[96,96]{1,0:T(8,128)S(1)} custom-call(f32[96,96]{1,0:T(8,128)S(1)} %convolution_subtract_fusion.1), custom_call_target="Cholesky" | custom-call | tf_op jit(solution)/shard_map/jit(cholesky)/cholesky | solution.py:46
  467.3 19.9 %custom-call.16 = f32[2,128,128]{1,2,0:T(8,128)S(1)} custom-call(f32[2,128,128]{2,1,0:T(8,128)S(1)} %pad_maximum_fusion.7), custom_call_target="InvertDiagBlocksLowerTriangular" | custom-call | tf_op jit(solution)/shard_map/jit(_solve_triangular)/triangular_solve | solution.py:48
  488.3 4.8 fusion.14
  493.1 1.3 fusion.20
  494.4 1.0 fusion.26
  495.4 3.6 copy.34
  (44 shorter events, 7.0 us)
Async XLA Ops:
  7.2 274.4 %all-reduce.6.cloned.1.call-start = ((), (), s32[]{:S(2)}) async-start(), calls=%async_computation | async-start | bytes 917504 | tf_op jit(solution)/shard_map/psum | solution.py:74
  18.0 25.3 %copy-start.1 = (s32[96,128]{1,0:T(8,128)S(1)}, s32[96,128]{1,0:T(8,128)}, u32[]{:S(2)}) copy-start(s32[96,128]{1,0:T(8,128)} %param.3) | copy-start | bytes 147460
  23.8 20.1 %collective-permute-start.1 = (bf16[224,96,2]{0,1,2:T(8,128)(2,1)S(1)}, bf16[224,96,2]{0,1,2:T(8,128)(2,1)S(1)}, u32[]{:S(2)}, u32[]{:S(2)}) collective-permute-start(bf16[224,96,2]{0,1,2:T(8,128)(2,1)S(1)} %copy.33), channel_id=1, source_target_pairs={{32,0},{64,32},{96,64},{128,96},{160,128},{192,160},{224,192},{33,... | collective-permute-start | bytes 258056 | tf_op jit(solution)/shard_map/ppermute | solution.py:15
  31.0 13.1 %collective-permute-start = (bf16[224,96,2]{0,1,2:T(8,128)(2,1)S(1)}, bf16[224,96,2]{0,1,2:T(8,128)(2,1)S(1)}, u32[]{:S(2)}, u32[]{:S(2)}) collective-permute-start(bf16[224,96,2]{0,1,2:T(8,128)(2,1)S(1)} %copy.32), channel_id=1, source_target_pairs={{0,32},{32,64},{64,96},{96,128},{128,160},{160,192},{192,224},{1,3... | collective-permute-start | bytes 258056 | tf_op jit(solution)/shard_map/ppermute | solution.py:12
  45.2 8.2 %collective-permute-start.2 = (bf16[224,2,132]{0,2,1:T(8,128)(2,1)S(1)}, bf16[224,2,132]{0,2,1:T(8,128)(2,1)S(1)}, u32[]{:S(2)}, u32[]{:S(2)}) collective-permute-start(bf16[224,2,132]{0,2,1:T(8,128)(2,1)S(1)} %get-tuple-element.26), channel_id=1, source_target_pairs={{0,1},{1,2},{2,3},{3,4},{4,5},{5,6},{6,7},{7,8},{8,9},{9,10},{10,1... | collective-permute-start | bytes 354824 | tf_op jit(solution)/shard_map/ppermute | solution.py:12
  49.0 10.5 %collective-permute-start.3 = (bf16[224,2,132]{0,2,1:T(8,128)(2,1)S(1)}, bf16[224,2,132]{0,2,1:T(8,128)(2,1)S(1)}, u32[]{:S(2)}, u32[]{:S(2)}) collective-permute-start(bf16[224,2,132]{0,2,1:T(8,128)(2,1)S(1)} %get-tuple-element.27), channel_id=1, source_target_pairs={{1,0},{2,1},{3,2},{4,3},{5,4},{6,5},{7,6},{8,7},{9,8},{10,9},{11,1... | collective-permute-start | bytes 354824 | tf_op jit(solution)/shard_map/ppermute | solution.py:15
  112.9 94.0 %slice-start = ((s8[6291456]{0:T(1024)(128)(4,1)}), s8[2097152]{0:T(1024)(128)(4,1)S(1)}, s32[]{:S(2)}) async-start(s8[6291456]{0:T(1024)(128)(4,1)} %bitcast.44), calls=%async_computation.2 | async-start | bytes 4194304
  193.0 13.9 %slice-start.1 = ((s8[6291456]{0:T(1024)(128)(4,1)}), s8[4194304]{0:T(1024)(128)(4,1)S(1)}, s32[]{:S(2)}) async-start(s8[6291456]{0:T(1024)(128)(4,1)} %bitcast.44), calls=%async_computation.3 | async-start | bytes 8388608
  210.2 220.0 %all-reduce.8.cloned.1.call-start = ((), (), s32[]{:S(2)}) async-start(), calls=%async_computation.1 | async-start | bytes 917504 | tf_op jit(solution)/shard_map/psum | solution.py:74
  430.2 62.9 %copy-start = (f32[224,448]{0,1:T(8,128)S(1)}, f32[224,448]{0,1:T(8,128)}, u32[]{:S(2)}) copy-start(f32[224,448]{0,1:T(8,128)} %all-reduce.8.cloned.1.call-done) | copy-start | bytes 1204228
Sparse Core Ops, SparseCore 0:
  210.3 71.2 all-reduce.5
  285.3 144.8 all-reduce.7
